TPU v7x, 32 devices: a whole 2x2x4 slice. The times are simulated.
32 devices in a mesh: agent: 8 (over y, x, core), res: 4 (over z).
Axes of the slice: x: 2, y: 2, z: 4, core: 2. Of those that a mesh axis runs over, the one named last changes fastest.
Arguments:
- linear_cost: float32 [2048, 2048], P('agent', 'res'), may hold values from -6 to 6
- agent_type: int32 [2048], P('agent'), may hold values from 0 to 3, as said below
- block_mask: int32 [2048, 16], P('agent', 'res'), may hold values 0 or 1
- inverses: bfloat16 [4, 2048, 2048], P(None, 'res'), as said below
- cost_weight: float32 [2048], P('res'), may hold values from 0.5 to 8
- target: float32 [2048], P('res'), may hold values from -6 to 6
Outputs:
- usage: float32 [2048, 2048], P('agent', 'res')
- shared: float32 [2048], P('res')
- prices: float32 [2048], P('res')
- primal_norm: float32 [5], replicated
- dual_norm: float32 [5], replicated
Inputs may be any that keep to these rules, and one draw needn't show every extreme that they name: Each inverses[k] is exactly symmetric: inverses[k, i, j] equals inverses[k, j, i]. `agent_type`: each aligned block of 256 agents (the agents held by one device along the agent axis) holds exactly 64 agents of each type, in no particular order.
All inputs are finite; a program needn't handle non-finite values. No bound on the sum of `block_mask` on one device may be relied on, other than what follows from the above.
Results may differ from a plain program's by a relative error of at most 0.0039.
Values may be sent and summed in bfloat16 or wider, within the bound.
No kernel may reach another device: no remote copies, remote signals or barrier semaphores. Data moves between devices by JAX's collectives and lax.ppermute only.
A program may use at most 64 MiB of HBM per device.

v0:
```python
import jax
import jax.numpy as jnp
from jax import lax
from jax.sharding import PartitionSpec as P

BLK = 128
ITERS = 5
penalty = 1.0
eps = 1e-06


def on_device(linear_cost, agent_type, block_mask, inverses, cost_weight, target):
    local_agents, local_width = linear_cost.shape
    type_count = inverses.shape[0]
    group_rows = local_agents // type_count
    count = local_agents * lax.axis_size("agent")
    block_count = block_mask.shape[1]
    order = jnp.argsort(agent_type, stable=True)
    restore = jnp.argsort(order, stable=True)
    expand = jnp.broadcast_to(
        block_mask.astype(jnp.float32)[:, :, None], (local_agents, block_count, BLK)
    ).reshape(local_agents, local_width)
    usage = jnp.zeros(linear_cost.shape, jnp.float32)
    mean_usage = jnp.zeros((local_width,), jnp.float32)
    shared = jnp.zeros((local_width,), jnp.float32)
    prices = jnp.zeros((local_width,), jnp.float32)
    primal_list = []
    dual_list = []
    for iteration in range(ITERS):
        rhs = (penalty * (usage - mean_usage + shared - prices) - linear_cost).astype(jnp.bfloat16)
        grouped = rhs[order].reshape(type_count, group_rows, local_width)
        product = jnp.einsum(
            "tas,tws->taw",
            lax.all_gather(grouped, "res", axis=2, tiled=True),
            inverses,
            preferred_element_type=jnp.float32,
        )
        new_usage = product.reshape(local_agents, local_width)[restore]
        new_usage = new_usage * expand
        change_local = penalty * penalty * jnp.sum((new_usage - usage) ** 2)
        usage = new_usage
        column_sum = jnp.sum(usage, axis=0)
        usage_sum = lax.psum(column_sum, "agent")
        dual2 = lax.psum(change_local, ("agent", "res"))
        mean_usage = usage_sum / count
        shared = (cost_weight * target + penalty * (prices + mean_usage)) / (cost_weight + penalty)
        prices = prices + mean_usage - shared
        primal2 = lax.psum(count * jnp.sum((mean_usage - shared) ** 2), "res")
        primal_list.append(jnp.sqrt(primal2 + eps))
        dual_list.append(jnp.sqrt(dual2 + eps))
    primal_norm = jnp.stack(primal_list)
    dual_norm = jnp.stack(dual_list)
    return (usage, shared, prices, primal_norm, dual_norm)


def solution(mesh):
    placed = (
        P("agent", "res"),
        P("agent"),
        P("agent", "res"),
        P(None, "res", None),
        P("res"),
        P("res"),
    )
    return jax.shard_map(
        on_device,
        mesh=mesh,
        in_specs=placed,
        out_specs=(P("agent", "res"), P("res"), P("res"), P(), P()),
        check_vma=False,
    )
```

profile of v0, /device:TPU:12, one launch (start us, length us, event | category | flops | bytes accessed | tf_op | source)
XLA Modules:
  0.0 334.9 jit_solution(6932095263842248031)
XLA Ops:
  7.2 0.0 all-gather.6.cloned.1.call-start
  7.2 3.8 %sort.31 = (s32[256]{0:T(256)}, s32[256]{0:T(256)S(1)}) sort(s32[256]{0:T(256)} %param.7, s32[256]{0:T(256)S(1)} %iota.7), dimensions={0}, to_apply=%region_0.0 | sort | flops 2048 | bytes 4096 | tf_op jit(solution)/shard_map/jit(argsort)/sort | solution.py:18
  11.1 1.1 subtract_convert_fusion.4
  12.2 1.9 gather_fusion
  14.0 0.0 all-gather.6.cloned.1.call-update
  14.0 0.0 all-gather.8.cloned.1.call-start
  14.1 3.2 sort.32
  17.3 0.7 convert_element_type.19
  18.0 0.1 copy.11
  18.1 0.0 copy-start.1
  18.1 0.0 copy-start.3
  18.1 0.0 copy-start
  18.2 25.1 %all-gather.6.cloned.1.call-done = bf16[4,64,2048]{2,1,0:T(8,128)(2,1)} async-done(((bf16[4,64,512]{2,1,0:T(8,128)(2,1)}), bf16[4,64,2048]{2,1,0:T(8,128)(2,1)}) %all-gather.6.cloned.1.call-update) | async-done | bytes 1048592 | tf_op jit(solution)/shard_map/all_gather | solution.py:34
  43.3 6.4 %fusion.13 = f32[4,64,512]{2,1,0:T(8,128)S(1)} fusion(bf16[4,64,2048]{2,1,0:T(8,128)(2,1)} %all-gather.6.cloned.1.call-done, bf16[4,512,2048]{2,1,0:T(8,128)(2,1)} %param.9), kind=kOutput, calls=%fused_computation.56 | convolution fusion | flops 536870912 | bytes 9961472 | tf_op jit(solution)/shard_map/tas,tws->taw/dot_general | solution.py:32
  49.7 1.0 gather_fusion.1
  50.7 0.3 broadcast_in_dim.11
  51.0 0.1 fusion.12
  51.1 11.9 %psum.105 = f32[512]{0:T(512)S(1)} all-reduce(f32[512]{0:T(512)S(1)} %get-tuple-element.44), channel_id=1, replica_groups=mesh['agent'=8,'res'=4] {'agent'}, use_global_device_ids=true, to_apply=%region_3.4 | all-reduce | flops 512 | bytes 4096 | tf_op jit(solution)/shard_map/psum | solution.py:43
  63.0 0.0 copy-done.3
  63.0 0.6 multiply_reduce_fusion.9
  63.6 0.1 subtract_convert_fusion.3
  63.7 1.9 gather_fusion.2
  65.6 0.0 all-gather.8.cloned.1.call-update
  65.6 0.0 all-gather.10.cloned.1.call-start
  65.7 27.5 %all-gather.8.cloned.1.call-done = bf16[4,64,2048]{2,1,0:T(8,128)(2,1)} async-done(((bf16[4,64,512]{2,1,0:T(8,128)(2,1)}), bf16[4,64,2048]{2,1,0:T(8,128)(2,1)}) %all-gather.8.cloned.1.call-update) | async-done | bytes 1048592 | tf_op jit(solution)/shard_map/all_gather | solution.py:34
  93.1 6.4 %fusion.14 = f32[4,64,512]{2,1,0:T(8,128)S(1)} fusion(bf16[4,64,2048]{2,1,0:T(8,128)(2,1)} %all-gather.8.cloned.1.call-done, bf16[4,512,2048]{2,1,0:T(8,128)(2,1)} %param.9), kind=kOutput, calls=%fused_computation.57 | convolution fusion | flops 536870912 | bytes 9961472 | tf_op jit(solution)/shard_map/tas,tws->taw/dot_general | solution.py:32
  99.5 1.0 gather_fusion.3
  100.5 0.1 fusion.11
  100.6 11.9 %psum.106 = f32[512]{0:T(512)S(1)} all-reduce(f32[512]{0:T(512)S(1)} %get-tuple-element.42), channel_id=1, replica_groups=mesh['agent'=8,'res'=4] {'agent'}, use_global_device_ids=true, to_apply=%region_5.6 | all-reduce | flops 512 | bytes 4096 | tf_op jit(solution)/shard_map/psum | solution.py:43
  112.5 0.6 multiply_reduce_fusion.8
  113.1 0.1 subtract_convert_fusion.2
  113.2 1.9 gather_fusion.4
  115.0 0.0 all-gather.10.cloned.1.call-update
  115.1 0.0 all-gather.12.cloned.1.call-start
  115.1 27.5 %all-gather.10.cloned.1.call-done = bf16[4,64,2048]{2,1,0:T(8,128)(2,1)} async-done(((bf16[4,64,512]{2,1,0:T(8,128)(2,1)}), bf16[4,64,2048]{2,1,0:T(8,128)(2,1)}) %all-gather.10.cloned.1.call-update) | async-done | bytes 1048592 | tf_op jit(solution)/shard_map/all_gather | solution.py:34
  142.6 6.4 %fusion.15 = f32[4,64,512]{2,1,0:T(8,128)S(1)} fusion(bf16[4,64,2048]{2,1,0:T(8,128)(2,1)} %all-gather.10.cloned.1.call-done, bf16[4,512,2048]{2,1,0:T(8,128)(2,1)} %param.9), kind=kOutput, calls=%fused_computation.58 | convolution fusion | flops 536870912 | bytes 9961472 | tf_op jit(solution)/shard_map/tas,tws->taw/dot_general | solution.py:32
  148.9 1.0 gather_fusion.5
  149.9 0.1 fusion.10
  150.0 12.1 %psum.107 = f32[512]{0:T(512)S(1)} all-reduce(f32[512]{0:T(512)S(1)} %get-tuple-element.40), channel_id=1, replica_groups=mesh['agent'=8,'res'=4] {'agent'}, use_global_device_ids=true, to_apply=%region_7.8 | all-reduce | flops 512 | bytes 4096 | tf_op jit(solution)/shard_map/psum | solution.py:43
  162.1 0.6 multiply_reduce_fusion.7
  162.7 0.1 subtract_convert_fusion.1
  162.8 1.9 gather_fusion.6
  164.7 0.0 all-gather.12.cloned.1.call-update
  164.7 0.0 all-gather.14.cloned.1.call-start
  164.8 27.4 %all-gather.12.cloned.1.call-done = bf16[4,64,2048]{2,1,0:T(8,128)(2,1)} async-done(((bf16[4,64,512]{2,1,0:T(8,128)(2,1)}), bf16[4,64,2048]{2,1,0:T(8,128)(2,1)}) %all-gather.12.cloned.1.call-update) | async-done | bytes 1048592 | tf_op jit(solution)/shard_map/all_gather | solution.py:34
  192.2 6.4 %fusion.16 = f32[4,64,512]{2,1,0:T(8,128)S(1)} fusion(bf16[4,64,2048]{2,1,0:T(8,128)(2,1)} %all-gather.12.cloned.1.call-done, bf16[4,512,2048]{2,1,0:T(8,128)(2,1)} %param.9), kind=kOutput, calls=%fused_computation.59 | convolution fusion | flops 536870912 | bytes 9961472 | tf_op jit(solution)/shard_map/tas,tws->taw/dot_general | solution.py:32
  198.6 1.8 gather_fusion.7
  200.4 1.2 fusion.9
  201.5 11.9 %psum.108 = f32[512]{0:T(512)S(1)} all-reduce(f32[512]{0:T(512)S(1)} %get-tuple-element.38), channel_id=1, replica_groups=mesh['agent'=8,'res'=4] {'agent'}, use_global_device_ids=true, to_apply=%region_9.10 | all-reduce | flops 512 | bytes 4096 | tf_op jit(solution)/shard_map/psum | solution.py:43
  213.4 0.6 multiply_reduce_fusion.6
  214.0 0.1 subtract_convert_fusion
  214.1 1.9 gather_fusion.8
  216.0 0.0 all-gather.14.cloned.1.call-update
  218.6 24.9 %all-gather.14.cloned.1.call-done = bf16[4,64,2048]{2,1,0:T(8,128)(2,1)} async-done(((bf16[4,64,512]{2,1,0:T(8,128)(2,1)}), bf16[4,64,2048]{2,1,0:T(8,128)(2,1)}) %all-gather.14.cloned.1.call-update) | async-done | bytes 1048592 | tf_op jit(solution)/shard_map/all_gather | solution.py:34
  243.5 6.4 %fusion.17 = f32[4,64,512]{2,1,0:T(8,128)S(1)} fusion(bf16[4,64,2048]{2,1,0:T(8,128)(2,1)} %all-gather.14.cloned.1.call-done, bf16[4,512,2048]{2,1,0:T(8,128)(2,1)} %param.9), kind=kOutput, calls=%fused_computation.60 | convolution fusion | flops 536870912 | bytes 9961472 | tf_op jit(solution)/shard_map/tas,tws->taw/dot_general | solution.py:32
  249.9 1.8 gather_fusion.9
  251.7 2.8 multiply_reduce_fusion
  254.5 11.9 %psum.109 = f32[512]{0:T(512)S(1)} all-reduce(f32[512]{0:T(512)S(1)} %get-tuple-element.14), channel_id=1, replica_groups=mesh['agent'=8,'res'=4] {'agent'}, use_global_device_ids=true, to_apply=%region_11.12 | all-reduce | flops 512 | bytes 4096 | tf_op jit(solution)/shard_map/psum | solution.py:43
  266.3 0.6 multiply_reduce_fusion.5
  267.6 0.6 fusion
  268.2 9.8 %all-reduce.1 = (f32[]{:T(128)}, f32[]{:T(128)}, f32[]{:T(128)}, f32[]{:T(128)}, f32[]{:T(128)}) all-reduce(f32[]{:T(128)S(6)} %mul.99, f32[]{:T(128)S(6)} %mul.100, f32[]{:T(128)S(6)} %mul.101, f32[]{:T(128)S(6)} %mul.102, f32[]{:T(128)S(6)} %mul.103), channel_id=1, replica_groups=mesh['agent'=8,'res'=4] {'res'}, use_global_device_ids=true, to_apply=%region_13.14 | all-reduce | flops 5 | bytes 40 | tf_op jit(solution)/shard_map/psum | solution.py:48
  281.3 42.5 %all-reduce = (f32[]{:T(128)}, f32[]{:T(128)}, f32[]{:T(128)}, f32[]{:T(128)}, f32[]{:T(128)}) all-reduce(f32[]{:T(128)} %get-tuple-element.13, f32[]{:T(128)} %get-tuple-element.12, f32[]{:T(128)} %get-tuple-element.11, f32[]{:T(128)} %get-tuple-element.10, f32[]{:T(128)} %get-tuple-element.9), channel_id=1, replica_groups=mesh['agent'=8,'res'=4] {'agent','res'}, use_global_device_ids=true, to_apply=%region_23.24 | all-reduce | flops 5 | bytes 40 | tf_op jit(solution)/shard_map/psum | solution.py:44
  327.2 0.6 stack.41
  327.8 0.6 stack.47
  (13 shorter events, 0.0 us)
Async XLA Ops:
  7.2 36.1 %all-gather.6.cloned.1.call-start = ((), (), s32[]{:S(2)}) async-start(), calls=%async_computation | async-start | bytes 1310720 | tf_op jit(solution)/shard_map/all_gather | solution.py:34
  14.0 79.1 %all-gather.8.cloned.1.call-start = ((), (), s32[]{:S(2)}) async-start(), calls=%async_computation.1 | async-start | bytes 1310720 | tf_op jit(solution)/shard_map/all_gather | solution.py:34
  18.1 44.9 %copy-start.1 = (f32[512]{0:T(512)S(1)}, f32[512]{0:T(512)}, u32[]{:S(2)}) copy-start(f32[512]{0:T(512)} %param.10) | copy-start | bytes 6148
  18.1 44.9 %copy-start.3 = (f32[512]{0:T(512)S(1)}, f32[512]{0:T(512)}, u32[]{:S(2)}) copy-start(f32[512]{0:T(512)} %param.11) | copy-start | bytes 6148
  18.1 45.5 %copy-start = (f32[256,512]{1,0:T(8,128)S(1)}, f32[256,512]{1,0:T(8,128)}, u32[]{:S(2)}) copy-start(f32[256,512]{1,0:T(8,128)} %param.6) | copy-start | bytes 1572868
  65.6 77.0 %all-gather.10.cloned.1.call-start = ((), (), s32[]{:S(2)}) async-start(), calls=%async_computation.2 | async-start | bytes 1310720 | tf_op jit(solution)/shard_map/all_gather | solution.py:34
  115.1 77.2 %all-gather.12.cloned.1.call-start = ((), (), s32[]{:S(2)}) async-start(), calls=%async_computation.3 | async-start | bytes 1310720 | tf_op jit(solution)/shard_map/all_gather | solution.py:34
  164.7 78.8 %all-gather.14.cloned.1.call-start = ((), (), s32[]{:S(2)}) async-start(), calls=%async_computation.4 | async-start | bytes 1310720 | tf_op jit(solution)/shard_map/all_gather | solution.py:34
  267.0 61.4 %copy-start.2 = (f32[512]{0:T(512)}, f32[512]{0:T(512)S(1)}, u32[]{:S(2)}) copy-start(f32[512]{0:T(512)S(1)} %get-tuple-element.26) | copy-start | bytes 6148
Sparse Core Ops, SparseCore 0:
  14.2 29.0 all-gather.5
  65.7 27.3 all-gather.7
  115.2 27.3 all-gather.9
  164.8 27.3 all-gather.11
  216.1 27.3 all-gather.13
where the time goes:
time: 336 us; the launch traced here: 335 us
  waiting for transfers between devices  132 us (39%)
  blocking collectives  112 us (33%)
  matrix products  31.9 us (9%)
  between operations  23.8 us (7%)
  local copies, waits for them, and re-layouts  17.4 us (5%)
  other arithmetic  17.3 us (5%)
    all_gather x5, waiting for transfers between devices, on_device(): lax.all_gather(grouped, 'res', axis=2, tiled=True)  132 us
    psum x5, blocking collectives, on_device(): usage_sum = lax.psum(column_sum, 'agent')  59.6 us
    psum x1, blocking collectives, on_device(): dual2 = lax.psum(change_local, ('agent', 'res'))  42.5 us
    dot_general x5, matrix products, on_device(): jnp.einsum('tas,tws->taw', lax.all_gather(grouped, 'res', axis=2, tiled=T...  31.9 us
    psum x1, blocking collectives, on_device(): primal2 = lax.psum(count * jnp.sum((mean_usage - shared) ** 2), 'res')  9.78 us
    gather x5, local copies, waits for them, and re-layouts, on_device(): grouped = rhs[order].reshape(type_count, group_rows, local_width)  9.27 us
  transfers between devices with their start and end apart: 5, of which 5 were waited for; matrix products, arithmetic and copies ran while one was open for 1% of the time, Pallas kernels for 0%

commit v1 on v0

--- a/solution.py
+++ b/solution.py
@@ -41,7 +41,12 @@
         usage = new_usage
         column_sum = jnp.sum(usage, axis=0)
         usage_sum = lax.psum(column_sum, "agent")
-        dual2 = lax.psum(change_local, ("agent", "res"))
+
+        def link_the_forms(own_rows):
+            res = lax.psum(own_rows, axis_name="agent")
+            return lax.psum(res, axis_name="res")
+
+        dual2 = link_the_forms(change_local)
         mean_usage = usage_sum / count
         shared = (cost_weight * target + penalty * (prices + mean_usage)) / (cost_weight + penalty)
         prices = prices + mean_usage - shared

time: 336 us -> 299 us (0.89); the launches traced: 335 us -> 294 us
  blocking collectives: 112 us -> 70.5 us
    psum x1 -> x0, blocking collectives: 42.5 us -> none  [on_device(): dual2 = lax.psum(change_local, ('agent', 'res'))]
where the time goes in v1:
time: 299 us; the launch traced here: 294 us
  waiting for transfers between devices  132 us (44%)
  blocking collectives  70.5 us (24%)
  matrix products  31.9 us (11%)
  between operations  23.8 us (8%)
  local copies, waits for them, and re-layouts  17.4 us (6%)
  other arithmetic  17.2 us (6%)
    all_gather x5, waiting for transfers between devices, on_device(): lax.all_gather(grouped, 'res', axis=2, tiled=True)  132 us
    psum x5, blocking collectives, on_device(): usage_sum = lax.psum(column_sum, 'agent')  60.5 us
    dot_general x5, matrix products, on_device(): jnp.einsum('tas,tws->taw', lax.all_gather(grouped, 'res', axis=2, tiled=T...  31.9 us
    psum x1, blocking collectives, on_device(): primal2 = lax.psum(count * jnp.sum((mean_usage - shared) ** 2), 'res')  10 us
    gather x5, local copies, waits for them, and re-layouts, on_device(): grouped = rhs[order].reshape(type_count, group_rows, local_width)  9.27 us
    gather x5, local copies, waits for them, and re-layouts, on_device(): new_usage = product.reshape(local_agents, local_width)[restore]  6.45 us
  transfers between devices with their start and end apart: 5, of which 5 were waited for; matrix products, arithmetic and copies ran while one was open for 1% of the time, Pallas kernels for 0%

profile of v1, /device:TPU:12, one launch (start us, length us, event | category | flops | bytes accessed | tf_op | source)
XLA Modules:
  0.0 293.5 jit_solution(14642825721862563443)
XLA Ops:
  7.2 0.0 all-gather.6.cloned.1.call-start
  7.2 3.8 %sort.31 = (s32[256]{0:T(256)}, s32[256]{0:T(256)S(1)}) sort(s32[256]{0:T(256)} %param.7, s32[256]{0:T(256)S(1)} %iota.7), dimensions={0}, to_apply=%region_0.0 | sort | flops 2048 | bytes 4096 | tf_op jit(solution)/shard_map/jit(argsort)/sort | solution.py:18
  11.1 1.1 subtract_convert_fusion.4
  12.2 1.9 gather_fusion
  14.0 0.0 all-gather.6.cloned.1.call-update
  14.0 0.0 all-gather.8.cloned.1.call-start
  14.1 3.2 %sort.32 = (s32[256]{0:T(256)}, s32[256]{0:T(256)S(1)}) sort(s32[256]{0:T(256)S(1)} %get-tuple-element.7, s32[256]{0:T(256)S(1)} %iota.8), dimensions={0}, to_apply=%region_1.2 | sort | flops 2048 | bytes 4096 | tf_op jit(solution)/shard_map/jit(argsort)/sort | solution.py:19
  17.3 0.7 convert_element_type.19
  18.0 0.1 copy.11
  18.1 0.0 copy-start.1
  18.1 0.0 copy-start.3
  18.1 0.0 copy-start
  18.2 25.1 %all-gather.6.cloned.1.call-done = bf16[4,64,2048]{2,1,0:T(8,128)(2,1)} async-done(((bf16[4,64,512]{2,1,0:T(8,128)(2,1)}), bf16[4,64,2048]{2,1,0:T(8,128)(2,1)}) %all-gather.6.cloned.1.call-update) | async-done | bytes 1048592 | tf_op jit(solution)/shard_map/all_gather | solution.py:34
  43.3 6.4 %fusion.13 = f32[4,64,512]{2,1,0:T(8,128)S(1)} fusion(bf16[4,64,2048]{2,1,0:T(8,128)(2,1)} %all-gather.6.cloned.1.call-done, bf16[4,512,2048]{2,1,0:T(8,128)(2,1)} %param.9), kind=kOutput, calls=%fused_computation.56 | convolution fusion | flops 536870912 | bytes 9961472 | tf_op jit(solution)/shard_map/tas,tws->taw/dot_general | solution.py:32
  49.7 1.0 gather_fusion.1
  50.7 0.3 broadcast_in_dim.11
  51.0 0.1 fusion.12
  51.1 11.9 %psum.140 = f32[512]{0:T(512)S(1)} all-reduce(f32[512]{0:T(512)S(1)} %get-tuple-element.50), channel_id=1, replica_groups=mesh['agent'=8,'res'=4] {'agent'}, use_global_device_ids=true, to_apply=%region_3.4 | all-reduce | flops 512 | bytes 4096 | tf_op jit(solution)/shard_map/psum | solution.py:43
  63.0 0.0 copy-done.1
  63.0 0.0 copy-done.3
  63.0 0.6 multiply_reduce_fusion.9
  63.6 0.1 subtract_convert_fusion.3
  63.7 1.9 gather_fusion.2
  65.6 0.0 all-gather.8.cloned.1.call-update
  65.6 0.0 all-gather.10.cloned.1.call-start
  65.7 27.5 %all-gather.8.cloned.1.call-done = bf16[4,64,2048]{2,1,0:T(8,128)(2,1)} async-done(((bf16[4,64,512]{2,1,0:T(8,128)(2,1)}), bf16[4,64,2048]{2,1,0:T(8,128)(2,1)}) %all-gather.8.cloned.1.call-update) | async-done | bytes 1048592 | tf_op jit(solution)/shard_map/all_gather | solution.py:34
  93.1 6.4 %fusion.14 = f32[4,64,512]{2,1,0:T(8,128)S(1)} fusion(bf16[4,64,2048]{2,1,0:T(8,128)(2,1)} %all-gather.8.cloned.1.call-done, bf16[4,512,2048]{2,1,0:T(8,128)(2,1)} %param.9), kind=kOutput, calls=%fused_computation.57 | convolution fusion | flops 536870912 | bytes 9961472 | tf_op jit(solution)/shard_map/tas,tws->taw/dot_general | solution.py:32
  99.5 1.0 gather_fusion.3
  100.5 0.1 fusion.11
  100.6 11.9 %psum.141 = f32[512]{0:T(512)S(1)} all-reduce(f32[512]{0:T(512)S(1)} %get-tuple-element.48), channel_id=1, replica_groups=mesh['agent'=8,'res'=4] {'agent'}, use_global_device_ids=true, to_apply=%region_5.6 | all-reduce | flops 512 | bytes 4096 | tf_op jit(solution)/shard_map/psum | solution.py:43
  112.5 0.6 multiply_reduce_fusion.8
  113.1 0.1 subtract_convert_fusion.2
  113.2 1.9 gather_fusion.4
  115.0 0.0 all-gather.10.cloned.1.call-update
  115.1 0.0 all-gather.12.cloned.1.call-start
  115.1 27.5 %all-gather.10.cloned.1.call-done = bf16[4,64,2048]{2,1,0:T(8,128)(2,1)} async-done(((bf16[4,64,512]{2,1,0:T(8,128)(2,1)}), bf16[4,64,2048]{2,1,0:T(8,128)(2,1)}) %all-gather.10.cloned.1.call-update) | async-done | bytes 1048592 | tf_op jit(solution)/shard_map/all_gather | solution.py:34
  142.6 6.4 %fusion.15 = f32[4,64,512]{2,1,0:T(8,128)S(1)} fusion(bf16[4,64,2048]{2,1,0:T(8,128)(2,1)} %all-gather.10.cloned.1.call-done, bf16[4,512,2048]{2,1,0:T(8,128)(2,1)} %param.9), kind=kOutput, calls=%fused_computation.58 | convolution fusion | flops 536870912 | bytes 9961472 | tf_op jit(solution)/shard_map/tas,tws->taw/dot_general | solution.py:32
  148.9 1.0 gather_fusion.5
  149.9 0.1 fusion.10
  150.0 12.1 %psum.142 = f32[512]{0:T(512)S(1)} all-reduce(f32[512]{0:T(512)S(1)} %get-tuple-element.46), channel_id=1, replica_groups=mesh['agent'=8,'res'=4] {'agent'}, use_global_device_ids=true, to_apply=%region_7.8 | all-reduce | flops 512 | bytes 4096 | tf_op jit(solution)/shard_map/psum | solution.py:43
  162.1 0.6 multiply_reduce_fusion.7
  162.7 0.1 subtract_convert_fusion.1
  162.8 1.9 gather_fusion.6
  164.7 0.0 all-gather.12.cloned.1.call-update
  164.7 0.0 all-gather.14.cloned.1.call-start
  164.8 27.4 %all-gather.12.cloned.1.call-done = bf16[4,64,2048]{2,1,0:T(8,128)(2,1)} async-done(((bf16[4,64,512]{2,1,0:T(8,128)(2,1)}), bf16[4,64,2048]{2,1,0:T(8,128)(2,1)}) %all-gather.12.cloned.1.call-update) | async-done | bytes 1048592 | tf_op jit(solution)/shard_map/all_gather | solution.py:34
  192.2 6.4 %fusion.16 = f32[4,64,512]{2,1,0:T(8,128)S(1)} fusion(bf16[4,64,2048]{2,1,0:T(8,128)(2,1)} %all-gather.12.cloned.1.call-done, bf16[4,512,2048]{2,1,0:T(8,128)(2,1)} %param.9), kind=kOutput, calls=%fused_computation.59 | convolution fusion | flops 536870912 | bytes 9961472 | tf_op jit(solution)/shard_map/tas,tws->taw/dot_general | solution.py:32
  198.6 1.8 gather_fusion.7
  200.4 1.2 fusion.9
  201.5 11.9 %psum.143 = f32[512]{0:T(512)S(1)} all-reduce(f32[512]{0:T(512)S(1)} %get-tuple-element.44), channel_id=1, replica_groups=mesh['agent'=8,'res'=4] {'agent'}, use_global_device_ids=true, to_apply=%region_9.10 | all-reduce | flops 512 | bytes 4096 | tf_op jit(solution)/shard_map/psum | solution.py:43
  213.4 0.6 multiply_reduce_fusion.6
  214.0 0.1 subtract_convert_fusion
  214.1 1.9 gather_fusion.8
  216.0 0.0 all-gather.14.cloned.1.call-update
  218.6 24.9 %all-gather.14.cloned.1.call-done = bf16[4,64,2048]{2,1,0:T(8,128)(2,1)} async-done(((bf16[4,64,512]{2,1,0:T(8,128)(2,1)}), bf16[4,64,2048]{2,1,0:T(8,128)(2,1)}) %all-gather.14.cloned.1.call-update) | async-done | bytes 1048592 | tf_op jit(solution)/shard_map/all_gather | solution.py:34
  243.5 6.4 %fusion.17 = f32[4,64,512]{2,1,0:T(8,128)S(1)} fusion(bf16[4,64,2048]{2,1,0:T(8,128)(2,1)} %all-gather.14.cloned.1.call-done, bf16[4,512,2048]{2,1,0:T(8,128)(2,1)} %param.9), kind=kOutput, calls=%fused_computation.60 | convolution fusion | flops 536870912 | bytes 9961472 | tf_op jit(solution)/shard_map/tas,tws->taw/dot_general | solution.py:32
  249.9 1.8 gather_fusion.9
  251.7 2.8 multiply_reduce_fusion
  254.4 12.8 %all-reduce = (f32[512]{0:T(512)S(1)}, f32[]{:T(128)}, f32[]{:T(128)}, f32[]{:T(128)}, f32[]{:T(128)}, /*index=5*/f32[]{:T(128)}) all-reduce(f32[512]{0:T(512)S(1)} %get-tuple-element.14, f32[]{:T(128)} %get-tuple-element.13, f32[]{:T(128)} %get-tuple-element.12, ...), channel_id=1, replica_groups=mesh['agent'=8,'res'=4] {'agent'}, use_global_device_ids=true, to_apply=%region_11.12 | all-reduce | flops 517 | bytes 4136 | tf_op jit(solution)/shard_map/psum | solution.py:43
  267.3 0.6 multiply_reduce_fusion.5
  268.5 0.6 fusion
  269.1 10.0 %all-reduce.1 = (f32[]{:T(128)}, f32[]{:T(128)}, f32[]{:T(128)}, f32[]{:T(128)}, f32[]{:T(128)}, /*index=5*/f32[]{:T(128)}, f32[]{:T(128)}, f32[]{:T(128)}, f32[]{:T(128)}, f32[]{:T(128)}) all-reduce(f32[]{:T(128)S(6)} %mul.99, f32[]{:T(128)S(6)} %mul.100, f32[]{:T(128)S(6)} %mul.101, ...), channel_id=1, replica_groups=mesh['agent'=8,'res'=4] {'res'}, use_global_device_ids=true, to_apply=%region_13.14 | all-reduce | flops 10 | bytes 80 | tf_op jit(solution)/shard_map/psum | solution.py:53
  285.8 0.6 stack.41
  286.4 0.6 stack.47
  (12 shorter events, 0.0 us)
Async XLA Ops:
  7.2 36.1 %all-gather.6.cloned.1.call-start = ((), (), s32[]{:S(2)}) async-start(), calls=%async_computation | async-start | bytes 1310720 | tf_op jit(solution)/shard_map/all_gather | solution.py:34
  14.0 79.1 %all-gather.8.cloned.1.call-start = ((), (), s32[]{:S(2)}) async-start(), calls=%async_computation.1 | async-start | bytes 1310720 | tf_op jit(solution)/shard_map/all_gather | solution.py:34
  18.1 44.9 %copy-start.1 = (f32[512]{0:T(512)S(1)}, f32[512]{0:T(512)}, u32[]{:S(2)}) copy-start(f32[512]{0:T(512)} %param.10) | copy-start | bytes 6148
  18.1 44.9 %copy-start.3 = (f32[512]{0:T(512)S(1)}, f32[512]{0:T(512)}, u32[]{:S(2)}) copy-start(f32[512]{0:T(512)} %param.11) | copy-start | bytes 6148
  18.1 45.5 %copy-start = (f32[256,512]{1,0:T(8,128)S(1)}, f32[256,512]{1,0:T(8,128)}, u32[]{:S(2)}) copy-start(f32[256,512]{1,0:T(8,128)} %param.6) | copy-start | bytes 1572868
  65.6 77.0 %all-gather.10.cloned.1.call-start = ((), (), s32[]{:S(2)}) async-start(), calls=%async_computation.2 | async-start | bytes 1310720 | tf_op jit(solution)/shard_map/all_gather | solution.py:34
  115.1 77.2 %all-gather.12.cloned.1.call-start = ((), (), s32[]{:S(2)}) async-start(), calls=%async_computation.3 | async-start | bytes 1310720 | tf_op jit(solution)/shard_map/all_gather | solution.py:34
  164.7 78.8 %all-gather.14.cloned.1.call-start = ((), (), s32[]{:S(2)}) async-start(), calls=%async_computation.4 | async-start | bytes 1310720 | tf_op jit(solution)/shard_map/all_gather | solution.py:34
  267.9 19.1 %copy-start.2 = (f32[512]{0:T(512)}, f32[512]{0:T(512)S(1)}, u32[]{:S(2)}) copy-start(f32[512]{0:T(512)S(1)} %get-tuple-element.32) | copy-start | bytes 6148
Sparse Core Ops, SparseCore 0:
  14.2 29.0 all-gather.5
  65.7 27.3 all-gather.7
  115.2 27.3 all-gather.9
  164.8 27.3 all-gather.11
  216.1 27.3 all-gather.13
